TPU v7x, 256 devices: a whole 4x4x8 slice. The times are simulated.
256 devices in a mesh: expert: 64 (over z, y, core), tensor: 4 (over x).
Axes of the slice: x: 4, y: 4, z: 8, core: 2. Of those that a mesh axis runs over, the one named last changes fastest.
Arguments:
- tokens: bfloat16 [8192, 2048], P('expert', 'tensor'), may hold values from -6 to 6
- grad_out: bfloat16 [8192, 2048], P('expert', 'tensor'), may hold values from -1.1953125 to 1.1953125
- routes: int32 [8192, 2], P('expert'), may hold values from 0 to 15, all different within a row; in each aligned block of 128 rows (0 to 127, 128 to 255, ...) at most 20 rows name the same one
- gates: float32 [8192, 2], P('expert'), may hold values from 0.1 to 1
- w_up: bfloat16 [2048, 131072], P(None, ('expert', 'tensor')), may hold values from -0.125 to 0.125
- w_down: bfloat16 [131072, 2048], P(('expert', 'tensor')), may hold values from -0.0625 to 0.0625
Outputs:
- grad_tokens: bfloat16 [8192, 2048], P('expert', 'tensor')
- grad_up: float32 [2048, 131072], P(None, ('expert', 'tensor'))
- grad_down: float32 [131072, 2048], P(('expert', 'tensor'))
Inputs may be any that keep to these rules, and one draw needn't show every extreme that they name: `routes`: the two experts of a token differ. Among the tokens of one index of the expert axis no expert is named more than 20 times, and in every draw some expert is named exactly 20 times by the tokens of some index.
All inputs are finite; a program needn't handle non-finite values.
Results may differ from a plain program's by a relative error of at most 0.012.
Values may be sent and summed in bfloat16 or wider, within the bound.
A program may use at most 128 MiB of HBM per device.

v0:
```python
import jax
import jax.numpy as jnp
from jax import lax
from jax.sharding import PartitionSpec as P

EXP_FULL = 16
root_half = 0.7071067811865476
gauss_norm = 0.3989422804014327


def split_up(x, dim, size):
    shape = x.shape
    tiles = x.reshape(*shape[:dim], size, shape[dim] // size, *shape[dim + 1 :])
    return jnp.moveaxis(tiles, dim, 0)


def sum_at_owner(x, axis, dim):
    size = lax.axis_size(axis)
    tiles = lax.all_to_all(split_up(x, dim, size), axis, 0, 0, tiled=True)
    return jnp.sum(tiles.astype(jnp.float32), axis=0)


def gelu_value(v):
    return 0.5 * v * (1.0 + lax.erf(v * root_half))


def gelu_slope(v):
    return 0.5 * (1.0 + lax.erf(v * root_half)) + v * jnp.exp(-0.5 * v * v) * gauss_norm


def local(tokens, grad_out, routes, gates, w_up, w_down):
    expert_count = lax.axis_size("expert")
    experts = min(EXP_FULL, expert_count)
    group = expert_count // experts
    tok_dev = routes.shape[0]
    choose = routes.shape[1]
    capacity = group * (5 * tok_dev // (2 * expert_count))
    flat = routes.reshape(-1)
    onehot = (flat[:, None] == jnp.arange(experts, dtype=jnp.int32)[None, :]).astype(jnp.int32)
    rank = jnp.cumsum(onehot, axis=0, dtype=jnp.int32) - onehot
    dest = flat * capacity + jnp.sum(rank * onehot, axis=1)
    select = (jnp.arange(experts * capacity, dtype=jnp.int32)[:, None] == dest[None, :]).astype(
        jnp.bfloat16
    )
    full_tok, full_grad = (tokens, grad_out)
    width = full_tok.shape[1]
    repeated = jnp.repeat(full_tok, choose, axis=0)
    scaled = (full_grad[:, None, :].astype(jnp.float32) * gates[:, :, None]).astype(jnp.bfloat16)
    scaled = scaled.reshape(tok_dev * choose, width)
    packed = (
        jnp.stack(
            [
                jnp.dot(select, repeated, preferred_element_type=jnp.float32),
                jnp.dot(select, scaled, preferred_element_type=jnp.float32),
            ]
        )
        .astype(jnp.bfloat16)
        .reshape(2, experts, capacity, width)
    )
    outgoing = jnp.repeat(packed, group, axis=1)
    arrived = lax.all_to_all(outgoing, "expert", split_axis=1, concat_axis=1, tiled=True)
    arrived = lax.all_gather(arrived, "tensor", axis=3, tiled=True)
    rows = arrived.reshape(2, expert_count * capacity, arrived.shape[3])
    rows_x = rows[0]
    rows_y = rows[1]
    pre = jnp.dot(rows_x, w_up, preferred_element_type=jnp.float32)
    act = gelu_value(pre).astype(jnp.bfloat16)
    d_act = lax.dot_general(
        rows_y, w_down, (((1,), (1,)), ((), ())), preferred_element_type=jnp.float32
    )
    d_pre = (d_act * gelu_slope(pre)).astype(jnp.bfloat16)
    grad_up = lax.dot_general(
        rows_x, d_pre, (((0,), (0,)), ((), ())), preferred_element_type=jnp.float32
    )
    grad_down = lax.dot_general(
        act, rows_y, (((0,), (0,)), ((), ())), preferred_element_type=jnp.float32
    )
    partial_value = lax.dot_general(
        d_pre, w_up, (((1,), (1,)), ((), ())), preferred_element_type=jnp.float32
    )
    partial_value = lax.optimization_barrier(partial_value.astype(jnp.bfloat16)).astype(jnp.float32)
    summed = sum_at_owner(partial_value.astype(jnp.bfloat16), "tensor", 1)
    quarter = summed.shape[1]
    back = summed.reshape(expert_count, capacity, quarter)
    returned = lax.all_to_all(
        back.astype(jnp.bfloat16), "expert", split_axis=0, concat_axis=0, tiled=True
    ).astype(back.dtype)
    combined = returned.reshape(experts, group, capacity, quarter).sum(axis=1)
    combined = combined.reshape(experts * capacity, quarter)
    grad_tokens = combined[dest].reshape(tok_dev, choose, quarter).sum(axis=1).astype(jnp.bfloat16)
    return (grad_tokens, grad_up, grad_down)


def solution(mesh):
    return jax.shard_map(
        local,
        mesh=mesh,
        in_specs=(
            P("expert", "tensor"),
            P("expert", "tensor"),
            P("expert", None),
            P("expert", None),
            P(None, ("expert", "tensor")),
            P(("expert", "tensor"), None),
        ),
        out_specs=(
            P("expert", "tensor"),
            P(None, ("expert", "tensor")),
            P(("expert", "tensor"), None),
        ),
        check_vma=False,
    )
```

profile of v0, /device:TPU:1, one launch (start us, length us, event | category | flops | bytes accessed | tf_op | source)
XLA Modules:
  0.0 406.1 jit_solution(18192644028344596392)
XLA Ops:
  7.2 0.0 copy-start
  7.2 0.0 all-gather.2.cloned.1.call-start
  7.2 0.9 copy.14
  8.2 0.1 eq.62
  8.3 0.1 reshape.145
  8.5 0.6 reduce-window.6
  9.0 0.2 slice_reduce_fusion.2
  9.3 0.1 fusion.20
  9.4 1.0 mul.84
  10.4 0.4 mul.85
  10.8 0.8 copy.17
  11.6 0.1 mul.86
  11.7 1.0 broadcast_in_dim.4
  12.8 0.1 reshape.164
  12.9 0.3 fusion.7
  13.2 0.3 fusion.8
  13.6 0.1 pad_maximum_fusion
  13.6 0.7 copy.18
  14.3 1.6 broadcast_in_dim.5
  15.9 75.8 %all_to_all.15 = bf16[2,64,20,512]{3,0,2,1:T(2,128)(2,1)} all-to-all(bf16[2,64,20,512]{3,0,2,1:T(2,128)(2,1)S(1)} %bitcast.52), channel_id=1, replica_groups=mesh['expert'=64,'tensor'=4] {'expert'}, dimensions={1} | all-to-all | bytes 5242880 | tf_op jit(solution)/shard_map/all_to_all | solution.py:61
  91.7 0.0 all-gather.2.cloned.1.call-update
  91.7 101.8 %all-gather.2.cloned.1.call-done = bf16[2,64,20,2048]{3,0,2,1:T(2,128)(2,1)} async-done(((bf16[2,64,20,512]{3,0,2,1:T(2,128)(2,1)}), bf16[2,64,20,2048]{3,0,2,1:T(2,128)(2,1)}) %all-gather.2.cloned.1.call-update) | async-done | bytes 10485776 | tf_op jit(solution)/shard_map/all_gather | solution.py:62
  193.5 52.4 %slice_reduce_fusion = (bf16[64,20,2048]{2,1,0:T(8,128)(2,1)}, bf16[64,20,2048]{2,1,0:T(8,128)(2,1)}) fusion(bf16[2,64,20,2048]{3,0,2,1:T(2,128)(2,1)} %all-gather.2.cloned.1.call-done), kind=kLoop, calls=%fused_computation.1 | loop fusion | bytes 20971520 | tf_op jit(solution)/shard_map/slice | solution.py:64
  245.9 9.0 %squeeze.7 = bf16[1280,2048]{1,0:T(8,128)(2,1)} reshape(bf16[64,20,2048]{2,1,0:T(8,128)(2,1)} %get-tuple-element.3) | data formatting | bytes 10485760 | tf_op jit(solution)/shard_map/squeeze | solution.py:64
  254.9 9.0 %squeeze.6 = bf16[1280,2048]{1,0:T(8,128)(2,1)} reshape(bf16[64,20,2048]{2,1,0:T(8,128)(2,1)} %get-tuple-element.4) | data formatting | bytes 10485760 | tf_op jit(solution)/shard_map/squeeze | solution.py:65
  263.9 0.0 copy-done
  263.9 0.0 copy-start.2
  263.9 0.0 copy-start.6
  263.9 4.9 %fusion.23 = f32[1280,512]{1,0:T(8,128)S(1)} fusion(bf16[1280,2048]{1,0:T(8,128)(2,1)} %squeeze.7, bf16[2048,512]{1,0:T(8,128)(2,1)S(1)} %copy-done), kind=kOutput, calls=%fused_computation.46 | convolution fusion | flops 2684354560 | bytes 9961472 | tf_op jit(solution)/shard_map/dot_general | solution.py:66
  268.8 0.0 copy-done.2
  268.8 0.0 copy-done.6
  268.9 0.0 copy-start.3
  268.9 3.9 fusion
  272.7 0.0 copy-done.3
  272.7 0.0 copy-start.7
  272.8 3.2 convolution_convert_fusion
  276.0 0.0 copy-done.7
  276.0 0.5 copy.27
  276.5 61.2 %all_to_all.16 = bf16[4,1280,512]{2,1,0:T(8,128)(2,1)} all-to-all(bf16[4,1280,512]{2,1,0:T(8,128)(2,1)S(1)} %bitcast.51), channel_id=1, replica_groups=mesh['expert'=64,'tensor'=4] {'tensor'}, dimensions={0} | all-to-all | bytes 10485760 | tf_op jit(solution)/shard_map/all_to_all | solution.py:19
  337.7 4.2 %reduce_sum.42 = bf16[1280,512]{1,0:T(8,128)(2,1)S(1)} reduce(bf16[4,1280,512]{2,1,0:T(8,128)(2,1)} %all_to_all.16, bf16[]{:T(256)} %constant.24.clone.1), dimensions={0}, to_apply=%region_3.4 | reduce | flops 1966080 | bytes 6553602 | tf_op jit(solution)/shard_map/reduce_sum | solution.py:20
  341.8 0.0 copy-start.5
  341.9 1.3 convert_element_type.46
  343.2 0.0 slice-start
  343.2 14.1 %all-to-all-start.2 = ((bf16[64,20,512]{2,1,0:T(8,128)(2,1)}), bf16[64,20,512]{2,1,0:T(8,128)(2,1)S(1)}, u32[]{:S(2)}, u32[]{:S(2)}) async-start(bf16[64,20,512]{2,1,0:T(8,128)(2,1)} %convert_element_type.46), calls=%async_computation.2 | async-start | bytes 3145728 | tf_op jit(solution)/shard_map/all_to_all | solution.py:85
  357.2 0.0 copy-done.5
  357.3 0.1 copy.20
  357.4 0.1 mul.100
  357.6 0.0 slice-start.1
  357.6 0.0 copy-start.4
  357.6 8.0 %fusion.24 = f32[2048,512]{1,0:T(8,128)} fusion(bf16[1280,2048]{1,0:T(8,128)(2,1)} %squeeze.7, bf16[1280,512]{1,0:T(8,128)(2,1)} %copy-done.7), kind=kOutput, calls=%fused_computation.47 | convolution fusion | flops 2684354560 | bytes 10747904 | tf_op jit(solution)/shard_map/dot_general | solution.py:72
  365.5 0.0 slice-done
  365.5 0.0 slice-done.1
  365.5 0.0 copy-done.4
  365.6 4.5 %fusion.5 = f32[512,2048]{1,0:T(8,128)} fusion(bf16[1280,2048]{1,0:T(8,128)(2,1)S(1)} %bitcast.50, f32[1280,512]{1,0:T(8,128)S(1)} %copy-done.4), kind=kOutput, calls=%fused_computation.15 | convolution fusion | flops 2687631360 | bytes 12058624 | tf_op jit(solution)/shard_map/dot_general | solution.py:75
  370.1 26.2 %all-to-all-done.2 = bf16[64,20,512]{2,1,0:T(8,128)(2,1)S(1)} async-done(((bf16[64,20,512]{2,1,0:T(8,128)(2,1)}), bf16[64,20,512]{2,1,0:T(8,128)(2,1)S(1)}, u32[]{:S(2)}, u32[]{:S(2)}) %all-to-all-start.2) | async-done | bytes 1310752 | tf_op jit(solution)/shard_map/all_to_all | solution.py:85
  396.3 0.3 convert_reduce_fusion
  396.6 0.0 copy-start.1
  396.6 0.1 reshape.152
  396.7 1.0 gather_fusion
  397.6 0.3 reshape.153
  397.9 1.3 reduce_sum.45
  399.3 0.0 copy-done.1
  (9 shorter events, 0.1 us)
Async XLA Ops:
  7.2 256.7 %copy-start = (bf16[2048,512]{1,0:T(8,128)(2,1)S(1)}, bf16[2048,512]{1,0:T(8,128)(2,1)}, u32[]{:S(2)}) copy-start(bf16[2048,512]{1,0:T(8,128)(2,1)} %param.10) | copy-start | bytes 6291460
  7.2 186.3 %all-gather.2.cloned.1.call-start = ((), (), s32[]{:S(2)}) async-start(), calls=%async_computation.3 | async-start | bytes 13107200 | tf_op jit(solution)/shard_map/all_gather | solution.py:62
  263.9 5.0 %copy-start.2 = (bf16[1280,2048]{1,0:T(8,128)(2,1)S(1)}, bf16[1280,2048]{1,0:T(8,128)(2,1)}, u32[]{:S(2)}) copy-start(bf16[1280,2048]{1,0:T(8,128)(2,1)} %squeeze.6) | copy-start | bytes 15728644
  263.9 5.0 %copy-start.6 = (bf16[512,2048]{1,0:T(8,128)(2,1)S(1)}, bf16[512,2048]{1,0:T(8,128)(2,1)}, u32[]{:S(2)}) copy-start(bf16[512,2048]{1,0:T(8,128)(2,1)} %param.11) | copy-start | bytes 6291460
  268.9 3.9 copy-start.3
  272.7 3.2 copy-start.7
  341.8 15.4 %copy-start.5 = (s32[128,2]{0,1:T(2,128)S(1)}, s32[128,2]{0,1:T(2,128)}, u32[]{:S(2)}) copy-start(s32[128,2]{0,1:T(2,128)} %param.8) | copy-start | bytes 3076
  343.2 22.4 %slice-start = ((s8[5242880]{0:T(1024)(128)(4,1)}), s8[1048576]{0:T(1024)(128)(4,1)S(1)}, s32[]{:S(2)}) async-start(s8[5242880]{0:T(1024)(128)(4,1)} %bitcast.49), calls=%async_computation.4 | async-start | bytes 2097152
  343.2 53.2 %all-to-all-start.2 = ((bf16[64,20,512]{2,1,0:T(8,128)(2,1)}), bf16[64,20,512]{2,1,0:T(8,128)(2,1)S(1)}, u32[]{:S(2)}, u32[]{:S(2)}) async-start(bf16[64,20,512]{2,1,0:T(8,128)(2,1)} %convert_element_type.46), calls=%async_computation.2 | async-start | bytes 3145728 | tf_op jit(solution)/shard_map/all_to_all | solution.py:85
  357.6 8.0 %slice-start.1 = ((s8[5242880]{0:T(1024)(128)(4,1)}), s8[4194304]{0:T(1024)(128)(4,1)S(1)}, s32[]{:S(2)}) async-start(s8[5242880]{0:T(1024)(128)(4,1)} %bitcast.49), calls=%async_computation.5 | async-start | bytes 8388608
  357.6 8.0 %copy-start.4 = (f32[1280,512]{1,0:T(8,128)S(1)}, f32[1280,512]{1,0:T(8,128)}, u32[]{:S(2)}) copy-start(f32[1280,512]{1,0:T(8,128)} %copy-done.3) | copy-start | bytes 7864324
  396.6 2.7 copy-start.1
Sparse Core Ops, SparseCore 0:
  91.9 101.5 all-gather.1
where the time goes:
time: 407 us; the launch traced here: 406 us
  blocking collectives  137 us (34%)
  waiting for transfers between devices  128 us (31%)
  local copies, waits for them, and re-layouts  81 us (20%)
  matrix products  25.2 us (6%)
  between operations  14.3 us (4%)
  starting transfers between devices  14.1 us (3%)
  other arithmetic  6.57 us (2%)
    all_gather x1, waiting for transfers between devices, local(): arrived = lax.all_gather(arrived, 'tensor', axis=3, tiled=True)  102 us
    all_to_all x1, blocking collectives, local(): lax.all_to_all(outgoing, 'expert', split_axis=1, concat_axis=1, tiled=True)  75.8 us
    all_to_all x1, blocking collectives, sum_at_owner(): tiles = lax.all_to_all(split_up(x, dim, size), axis, 0, 0, tiled=True)  61.2 us
    slice x1, local copies, waits for them, and re-layouts, local(): rows_x = rows[0]  52.4 us
    all_to_all x1, waiting for transfers between devices, local(): lax.all_to_all(back.astype(jnp.bfloat16), 'expert', split_axis=0, concat_...  26.2 us
    all_to_all x1, starting transfers between devices, local(): lax.all_to_all(back.astype(jnp.bfloat16), 'expert', split_axis=0, concat_...  14.1 us
    squeeze x1, local copies, waits for them, and re-layouts, local(): rows_y = rows[1]  9 us
    squeeze x1, local copies, waits for them, and re-layouts, local(): rows_x = rows[0]  8.99 us
  transfers between devices with their start and end apart: 2, of which 2 were waited for; matrix products, arithmetic and copies ran while one was open for 3% of the time, Pallas kernels for 0%

commit v1 on v0

--- a/solution.py
+++ b/solution.py
@@ -59,7 +59,9 @@
     )
     outgoing = jnp.repeat(packed, group, axis=1)
     arrived = lax.all_to_all(outgoing, "expert", split_axis=1, concat_axis=1, tiled=True)
-    arrived = lax.all_gather(arrived, "tensor", axis=3, tiled=True)
+    arrived = jnp.concatenate(
+        lax.all_to_all(jnp.stack([arrived] * lax.axis_size("tensor")), "tensor", 0, 0), axis=3
+    )
     rows = arrived.reshape(2, expert_count * capacity, arrived.shape[3])
     rows_x = rows[0]
     rows_y = rows[1]

time: 407 us -> 378 us (0.929)
  blocking collectives: 137 us -> 263 us
  waiting for transfers between devices: 128 us -> 26.2 us
  local copies, waits for them, and re-layouts: 81 us -> 48.9 us
  between operations: 14.3 us -> 0.95 us
  starting transfers between devices: 14.1 us -> 7.05 us
    all_to_all x0 -> x1, blocking collectives: none -> 124 us  [local(): lax.all_to_all(jnp.stack([arrived] * lax.axis_size('tensor')), 'tensor',...]
    all_gather x1 -> x0, waiting for transfers between devices: 102 us -> none  [local(): arrived = lax.all_gather(arrived, 'tensor', axis=3, tiled=True)]
    slice x1 -> x2, local copies, waits for them, and re-layouts: 52.4 us -> 16.3 us  [local(): rows_x = rows[0]]
    squeeze x2 -> x0, local copies, waits for them, and re-layouts: 18 us -> none  [the longest x1 9 us: local(): rows_y = rows[1]]
    unnamed x22 -> x28, local copies, waits for them, and re-layouts: 1.77 us -> 10.3 us
    all_to_all x1, starting transfers between devices: 14.1 us -> 7.05 us  [local(): lax.all_to_all(back.astype(jnp.bfloat16), 'expert', split_axis=0, concat_...]
    another operation x1 -> x2, local copies, waits for them, and re-layouts: 0.01 us -> 6.91 us  [the longest x1 6.91 us: local(): jnp.stack([arrived] * lax.axis_size('tensor'))]
  transfers between devices with their start and end apart: 2 -> 1, of which waited for: 2 -> 1; matrix products, arithmetic and copies ran while one was open for 3% -> 3% of each run, Pallas kernels for 0% -> 0%
where the time goes in v1:
time: 378 us; the launch traced here: 377 us
  blocking collectives  263 us (70%)
  local copies, waits for them, and re-layouts  48.9 us (13%)
  waiting for transfers between devices  26.2 us (7%)
  matrix products  23.2 us (6%)
  other arithmetic  8.06 us (2%)
  starting transfers between devices  7.05 us (2%)
    all_to_all x1, blocking collectives, local(): lax.all_to_all(jnp.stack([arrived] * lax.axis_size('tensor')), 'tensor',...  124 us
    all_to_all x1, blocking collectives, local(): lax.all_to_all(outgoing, 'expert', split_axis=1, concat_axis=1, tiled=True)  75.7 us
    all_to_all x1, blocking collectives, sum_at_owner(): tiles = lax.all_to_all(split_up(x, dim, size), axis, 0, 0, tiled=True)  62.5 us
    all_to_all x1, waiting for transfers between devices, local(): lax.all_to_all(back.astype(jnp.bfloat16), 'expert', split_axis=0, concat_...  26.2 us
    slice x2, local copies, waits for them, and re-layouts, local(): rows_x = rows[0]  16.3 us
    unnamed x28, local copies, waits for them, and re-layouts  10.3 us
    dot_general x1, matrix products, local(): lax.dot_general(rows_x, d_pre, (((0,), (0,)), ((), ())), preferred_elemen...  7.96 us
  transfers between devices with their start and end apart: 1, of which 1 were waited for; matrix products, arithmetic and copies ran while one was open for 3% of the time, Pallas kernels for 0%

profile of v1, /device:TPU:1, one launch (start us, length us, event | category | flops | bytes accessed | tf_op | source)
XLA Modules:
  0.0 377.0 jit_solution(13304551178562915950)
XLA Ops:
  0.6 0.0 copy-start
  0.7 0.9 copy.24
  1.6 0.1 reshape.149
  1.7 0.1 eq.62
  1.9 0.6 reduce-window.6
  2.5 0.2 slice_reduce_fusion
  2.7 0.1 fusion.20
  2.8 0.8 copy.27
  3.6 0.1 mul.86
  3.7 1.0 broadcast_in_dim.4
  4.8 0.1 reshape.169
  4.9 1.0 mul.84
  5.9 0.4 mul.85
  6.3 0.3 fusion.7
  6.6 0.3 fusion.8
  7.0 0.1 pad_maximum_fusion
  7.1 0.7 copy.28
  7.8 1.6 broadcast_in_dim.5
  9.4 75.7 %all_to_all.20 = bf16[2,64,20,512]{3,0,2,1:T(2,128)(2,1)S(1)} all-to-all(bf16[2,64,20,512]{3,0,2,1:T(2,128)(2,1)S(1)} %bitcast.66), channel_id=1, replica_groups=mesh['expert'=64,'tensor'=4] {'expert'}, dimensions={1} | all-to-all | bytes 5242880 | tf_op jit(solution)/shard_map/all_to_all | solution.py:61
  85.0 2.4 copy.29
  87.4 6.9 %stack.5 = bf16[4,2,64,20,512]{4,2,3,1,0:T(8,128)(2,1)} broadcast(bf16[2,64,20,512]{3,1,2,0:T(8,128)(2,1)} %copy.29), dimensions={1,2,3,4} | broadcast | bytes 13107200 | tf_op jit(solution)/shard_map/stack | solution.py:63
  94.3 124.5 %all_to_all.21 = bf16[4,2,64,20,512]{4,2,3,1,0:T(8,128)(2,1)} all-to-all(bf16[4,2,64,20,512]{4,2,3,1,0:T(8,128)(2,1)} %stack.5), channel_id=1, replica_groups=mesh['expert'=64,'tensor'=4] {'tensor'}, dimensions={0} | all-to-all | bytes 20971520 | tf_op jit(solution)/shard_map/all_to_all | solution.py:63
  218.8 9.6 %fusion.23 = (bf16[1,64,20,4,512]{4,1,2,0,3:T(8,128)(2,1)}, bf16[1,64,20,4,512]{4,1,2,0,3:T(8,128)(2,1)}) fusion(bf16[2,64,20,4,512]{4,1,2,0,3:T(8,128)(2,1)} %bitcast.56), kind=kLoop, calls=%fused_computation.44 | loop fusion | bytes 20971520 | tf_op jit(solution)/shard_map/slice | solution.py:66
  228.5 6.7 %copy.31 = bf16[1,64,20,4,512]{4,3,2,1,0:T(4,128)(2,1)S(1)} copy(bf16[1,64,20,4,512]{4,1,2,0,3:T(8,128)(2,1)} %get-tuple-element.3) | data formatting | bytes 10485760 | tf_op jit(solution)/shard_map/slice | solution.py:66
  235.1 0.0 slice-start.3
  235.2 4.6 %copy.37 = bf16[160,8,4,512]{3,1,2,0:T(8,128)(2,1)} copy(bf16[160,8,4,512]{3,2,1,0:T(4,128)(2,1)S(1)} %bitcast.63) | data formatting | bytes 10485760
  239.7 0.0 slice-done.2
  239.7 0.0 slice-done.3
  239.7 4.0 %copy.30 = bf16[1,64,20,4,512]{4,3,2,1,0:T(4,128)(2,1)S(1)} copy(bf16[1,64,20,4,512]{4,1,2,0,3:T(8,128)(2,1)S(1)} %bitcast.62) | data formatting | bytes 10485760 | tf_op jit(solution)/shard_map/slice | solution.py:67
  243.8 0.0 copy-start.4
  243.8 2.5 copy.36
  246.3 0.0 copy-start.1
  246.3 0.0 copy-done
  246.3 0.0 copy-done.4
  246.3 0.0 copy-start.6
  246.3 2.9 fusion.24
  249.3 0.0 copy-start.2
  249.3 0.0 copy-done.1
  249.3 1.5 copy-done.2
  250.8 0.0 copy-done.6
  250.8 3.9 %fusion = bf16[1280,512]{1,0:T(8,128)(2,1)S(1)} fusion(bf16[1280,2048]{1,0:T(8,128)(2,1)S(1)} %bitcast.57, bf16[512,2048]{1,0:T(8,128)(2,1)S(1)} %copy-done.6, f32[1280,512]{1,0:T(8,128)S(1)} %fusion.24), kind=kOutput, calls=%fused_computation.6 | convolution fusion | flops 2690908160 | bytes 11272192 | tf_op jit(solution)/shard_map/dot_general | solution.py:70
  254.7 0.0 copy-start.7
  254.7 3.2 convolution_convert_fusion
  257.9 0.0 copy-done.7
  257.9 0.5 copy.40
  258.4 62.5 %all_to_all.22 = bf16[4,1280,512]{2,1,0:T(8,128)(2,1)} all-to-all(bf16[4,1280,512]{2,1,0:T(8,128)(2,1)S(1)} %bitcast.65), channel_id=1, replica_groups=mesh['expert'=64,'tensor'=4] {'tensor'}, dimensions={0} | all-to-all | bytes 10485760 | tf_op jit(solution)/shard_map/all_to_all | solution.py:19
  320.9 4.2 %reduce_sum.42 = bf16[1280,512]{1,0:T(8,128)(2,1)S(1)} reduce(bf16[4,1280,512]{2,1,0:T(8,128)(2,1)} %all_to_all.22, bf16[]{:T(256)} %constant.24.clone.1), dimensions={0}, to_apply=%region_3.4 | reduce | flops 1966080 | bytes 6553602 | tf_op jit(solution)/shard_map/reduce_sum | solution.py:20
  325.1 0.0 copy-start.5
  325.1 1.4 convert_element_type.46
  326.5 7.1 %all-to-all-start.3 = ((bf16[64,20,512]{2,1,0:T(8,128)(2,1)}), bf16[64,20,512]{2,1,0:T(8,128)(2,1)}, u32[]{:S(2)}, u32[]{:S(2)}) async-start(bf16[64,20,512]{2,1,0:T(8,128)(2,1)} %convert_element_type.46), calls=%async_computation.3 | async-start | bytes 3145728 | tf_op jit(solution)/shard_map/all_to_all | solution.py:87
  333.5 0.1 copy.33
  333.6 0.1 mul.100
  333.8 0.0 slice-start.1
  333.8 0.0 copy-start.3
  333.8 8.0 %fusion.25 = f32[2048,512]{1,0:T(8,128)} fusion(bf16[1280,2048]{1,0:T(8,128)(2,1)} %bitcast.67, bf16[1280,512]{1,0:T(8,128)(2,1)} %copy-done.7), kind=kOutput, calls=%fused_computation.46 | convolution fusion | flops 2684354560 | bytes 10747904 | tf_op jit(solution)/shard_map/dot_general | solution.py:74
  341.8 0.0 slice-done
  341.8 0.0 copy-done.3
  341.8 4.5 %fusion.5 = f32[512,2048]{1,0:T(8,128)} fusion(bf16[1280,2048]{1,0:T(8,128)(2,1)S(1)} %bitcast.60, f32[1280,512]{1,0:T(8,128)S(1)} %copy-done.3), kind=kOutput, calls=%fused_computation.13 | convolution fusion | flops 2687631360 | bytes 12058624 | tf_op jit(solution)/shard_map/dot_general | solution.py:77
  346.4 26.2 %all-to-all-done.3 = bf16[64,20,512]{2,1,0:T(8,128)(2,1)} async-done(((bf16[64,20,512]{2,1,0:T(8,128)(2,1)}), bf16[64,20,512]{2,1,0:T(8,128)(2,1)}, u32[]{:S(2)}, u32[]{:S(2)}) %all-to-all-start.3) | async-done | bytes 1310752 | tf_op jit(solution)/shard_map/all_to_all | solution.py:87
  372.6 1.7 convert_reduce_fusion
  374.3 0.1 reshape.157
  374.4 1.0 gather_fusion
  375.4 0.3 reshape.158
  375.7 1.3 reduce_sum.45
  (14 shorter events, 0.1 us)
Async XLA Ops:
  0.6 245.7 %copy-start = (bf16[2048,512]{1,0:T(8,128)(2,1)S(1)}, bf16[2048,512]{1,0:T(8,128)(2,1)}, u32[]{:S(2)}) copy-start(bf16[2048,512]{1,0:T(8,128)(2,1)} %param.10) | copy-start | bytes 6291460
  228.5 11.3 %slice-start.2 = ((s8[5242880]{0:T(1024)(128)(4,1)}), s8[4194304]{0:T(1024)(128)(4,1)S(1)}, s32[]{:S(2)}) async-start(s8[5242880]{0:T(1024)(128)(4,1)} %bitcast.61), calls=%async_computation.6 | async-start | bytes 8388608
  235.1 4.6 %slice-start.3 = ((s8[5242880]{0:T(1024)(128)(4,1)}), s8[1048576]{0:T(1024)(128)(4,1)S(1)}, s32[]{:S(2)}) async-start(s8[5242880]{0:T(1024)(128)(4,1)} %bitcast.61), calls=%async_computation.7 | async-start | bytes 2097152
  243.8 2.6 copy-start.4
  246.3 3.0 copy-start.1
  246.3 4.4 %copy-start.6 = (bf16[512,2048]{1,0:T(8,128)(2,1)S(1)}, bf16[512,2048]{1,0:T(8,128)(2,1)}, u32[]{:S(2)}) copy-start(bf16[512,2048]{1,0:T(8,128)(2,1)} %param.11) | copy-start | bytes 6291460
  249.3 1.5 copy-start.2
  254.7 3.2 copy-start.7
  325.1 8.5 %copy-start.5 = (s32[128,2]{0,1:T(2,128)S(1)}, s32[128,2]{0,1:T(2,128)}, u32[]{:S(2)}) copy-start(s32[128,2]{0,1:T(2,128)} %param.8) | copy-start | bytes 3076
  326.4 15.4 %slice-start = ((s8[5242880]{0:T(1024)(128)(4,1)}), s8[1048576]{0:T(1024)(128)(4,1)S(1)}, s32[]{:S(2)}) async-start(s8[5242880]{0:T(1024)(128)(4,1)} %bitcast.58), calls=%async_computation.4 | async-start | bytes 2097152
  326.5 46.1 %all-to-all-start.3 = ((bf16[64,20,512]{2,1,0:T(8,128)(2,1)}), bf16[64,20,512]{2,1,0:T(8,128)(2,1)}, u32[]{:S(2)}, u32[]{:S(2)}) async-start(bf16[64,20,512]{2,1,0:T(8,128)(2,1)} %convert_element_type.46), calls=%async_computation.3 | async-start | bytes 3145728 | tf_op jit(solution)/shard_map/all_to_all | solution.py:87
  333.8 8.0 %slice-start.1 = ((s8[5242880]{0:T(1024)(128)(4,1)}), s8[4194304]{0:T(1024)(128)(4,1)S(1)}, s32[]{:S(2)}) async-start(s8[5242880]{0:T(1024)(128)(4,1)} %bitcast.58), calls=%async_computation.5 | async-start | bytes 8388608
  333.8 8.0 %copy-start.3 = (f32[1280,512]{1,0:T(8,128)S(1)}, f32[1280,512]{1,0:T(8,128)}, u32[]{:S(2)}) copy-start(f32[1280,512]{1,0:T(8,128)} %copy-done.2) | copy-start | bytes 7864324
